TPU v7x, 256 devices: a whole 4x4x8 slice. The times are simulated.
256 devices in a mesh: sec: 64 (over y, z, core), reg: 4 (over x).
Axes of the slice: x: 4, y: 4, z: 8, core: 2. Of those that a mesh axis runs over, the one named last changes fastest.
Arguments:
- start_params: float32 [64, 4, 20, 128], P('sec', 'reg'), may hold values from -3 to 3
- right_side: float32 [64, 4, 20, 128], P('sec', 'reg'), may hold values from -40 to 40
- prior: float32 [64, 4, 20, 128], P('sec', 'reg'), may hold values from 0.1 to 1
- matches: bfloat16 [64, 4, 640, 4, 256], P('sec', 'reg'), may hold values from -1 to 1
- pair_first: int32 [64, 4, 640], P('sec', 'reg'), may hold values from 0 to 127, as said below
- pair_second: int32 [64, 4, 640], P('sec', 'reg'), may hold values from 0 to 415, as said below
- match_counts: int32 [64, 4, 640], P('sec', 'reg'), may hold values from 0 to 256, as said below
- send_lists: int32 [64, 4, 2, 16], P('sec', 'reg'), may hold values from 0 to 127, as said below
Outputs:
- solution: float32 [64, 4, 20, 128], P('sec', 'reg')
- residual: float32 [64, 4, 20, 128], P('sec', 'reg')
Inputs may be any that keep to these rules, and one draw needn't show every extreme that they name: Each tile is pair_first of exactly five pairs of its device, in a drawn order. `pair_second`: names a column of the extended field; blocks of neighbours outside the grid are never named; a pair with match count 0 names its own tile. `match_counts`: 0 marks an absent pair; every device has a pair with exactly 256 matches. `send_lists`: row 0 holds the tiles whose coefficients a region lends to the region below it, row 1 to the region above; each row has 16 distinct tiles and the rows are disjoint.
All inputs are finite; a program needn't handle non-finite values.
Results may differ from a plain program's by a relative error of at most 0.0003.
Values sent between devices are 32-bit elements; how exact they have to be, the bound alone decides.
A program may use at most 64 MiB of HBM per device.

v0:
```python
import math
import jax
import jax.numpy as jnp
from jax import lax
from jax.sharding import PartitionSpec as P

FULL_PRECISION = lax.Precision.HIGHEST


def shifted(array, axis, by):
    length = lax.axis_size(axis)
    pairs = [(i, i + by) for i in range(length) if 0 <= i + by < length]
    return lax.ppermute(array, axis, pairs)


def padded_2(array, sides, width):
    for axis, dim in sides:
        size, length = (lax.axis_size(axis), array.shape[dim])
        up = [(i, (i + 1) % size) for i in range(size - 1)]
        down = [(j, i) for i, j in up]
        last = lax.slice_in_dim(array, length - width, length, axis=dim)
        first = lax.slice_in_dim(array, 0, width, axis=dim)
        before = lax.ppermute(last, axis, up)
        after = lax.ppermute(first, axis, down)
        array = jnp.concatenate([before, array, after], axis=dim)
    return array


def monomials(across, upward):
    constant = jnp.ones_like(across)
    square_a = across * across
    square_b = upward * upward
    mixed = across * upward
    return jnp.stack(
        [
            constant,
            across,
            upward,
            square_a,
            mixed,
            square_b,
            square_a * across,
            square_a * upward,
            square_b * across,
            square_b * upward,
        ]
    )


def match_bases(count_blk, match_blk):
    points = match_blk.astype(jnp.float32)
    slots = points.shape[-1]
    basis_a = monomials(points[:, 0], points[:, 1])
    basis_b = monomials(points[:, 2], points[:, 3])
    weights = jnp.where(jnp.arange(slots)[None, :] < count_blk[:, None], 2.0 / slots, 0.0).astype(
        jnp.float32
    )
    return (basis_a, basis_b, weights)


def block_terms(extended, first_blk, second_blk, count_blk, match_blk):
    width = first_blk.shape[0]
    basis_a, basis_b, weights = match_bases(count_blk, match_blk)
    own = jnp.take(extended, first_blk, axis=1).reshape(2, 10, width)
    other = jnp.take(extended, second_blk, axis=1).reshape(2, 10, width)
    mismatch = (
        jnp.einsum("mpk,cmp->cpk", basis_a, own, precision=FULL_PRECISION)
        - jnp.einsum("mpk,cmp->cpk", basis_b, other, precision=FULL_PRECISION)
    ) * weights[None]
    to_own = jnp.einsum("mpk,cpk->cmp", basis_a, mismatch, precision=FULL_PRECISION).reshape(
        20, width
    )
    to_other = -jnp.einsum("mpk,cpk->cmp", basis_b, mismatch, precision=FULL_PRECISION).reshape(
        20, width
    )
    return (to_own, to_other)


def split_blocks(first, second, counts, matches):
    pairs = first.shape[0]
    block = math.gcd(pairs, 512)
    blocks = pairs // block
    slots = matches.shape[-1]
    return (
        first.reshape(blocks, block),
        second.reshape(blocks, block),
        counts.reshape(blocks, block),
        matches.reshape(blocks, block, 4, slots),
    )


def extend(params, send_lists):
    arrived = params
    taken = []
    for hop_index in range(2):
        arrived = shifted(arrived, "sec", 1)
        taken.append(arrived)
    near_params, far_params = (taken[0], taken[1])
    faces = jnp.stack(
        [jnp.take(params, send_lists[0], axis=1), jnp.take(params, send_lists[1], axis=1)]
    )
    padded = padded_2(faces, (("reg", 0),), 1)
    return jnp.concatenate([params, near_params, far_params, padded[0], padded[3]], axis=1)


def fold_back(products, tiles, rows, send_lists):
    local = products[:, :tiles]
    near_part = products[:, tiles : 2 * tiles]
    far_part = products[:, 2 * tiles : 3 * tiles]
    outgoing = far_part
    arrived = far_part
    for hop_index in range(2):
        arrived = shifted(outgoing, "sec", -1)
        outgoing = near_part + arrived
    local = local + arrived
    faces = jnp.stack([products[:, 3 * tiles : 3 * tiles + rows], products[:, 3 * tiles + rows :]])
    padded = padded_2(faces, (("reg", 0),), 1)
    local = local.at[:, send_lists[0]].add(padded[0])
    return local.at[:, send_lists[1]].add(padded[3])


def apply_normal(params, prior, first, second, counts, matches, send_lists):
    tiles = params.shape[1]
    rows = send_lists.shape[1]
    pairs = first.shape[0]
    extended = extend(params, send_lists)
    pieces = split_blocks(first, second, counts, matches)
    to_own, to_other = lax.map(
        lambda items: block_terms(extended, items[0], items[1], items[2], items[3]), pieces
    )
    to_own = jnp.moveaxis(to_own, 0, 1).reshape(20, pairs)
    to_other = jnp.moveaxis(to_other, 0, 1).reshape(20, pairs)
    products = jnp.zeros((20, extended.shape[1]), jnp.float32)
    products = products.at[:, first].add(to_own).at[:, second].add(to_other)
    return fold_back(products, tiles, rows, send_lists) + prior * params


def global_dot(value):
    return lax.psum(value, ("sec", "reg"))


def on_device(
    start_params, right_side, prior, matches, pair_first, pair_second, match_counts, send_lists
):
    params_start = start_params[0, 0]
    target = right_side[0, 0]
    damping = prior[0, 0]
    first = pair_first[0, 0]
    second = pair_second[0, 0]
    counts = match_counts[0, 0]
    points = matches[0, 0]
    border = send_lists[0, 0]

    def normal(field):
        return apply_normal(field, damping, first, second, counts, points, border)

    solution = params_start
    residual = target - normal(params_start)
    direction = residual
    norm_now = global_dot(jnp.sum(residual * residual))
    image = normal(direction)
    alpha = norm_now / global_dot(jnp.sum(direction * image))
    solution = solution + alpha * direction
    residual = residual - alpha * image
    return (solution[None, None], residual[None, None])


def solution(mesh):
    return jax.shard_map(
        on_device,
        mesh=mesh,
        in_specs=(
            P("sec", "reg", None, None),
            P("sec", "reg", None, None),
            P("sec", "reg", None, None),
            P("sec", "reg", None, None, None),
            P("sec", "reg", None),
            P("sec", "reg", None),
            P("sec", "reg", None),
            P("sec", "reg", None, None),
        ),
        out_specs=(P("sec", "reg", None, None), P("sec", "reg", None, None)),
        check_vma=False,
    )
```

profile of v0, /device:TPU:1, one launch (start us, length us, event | category | flops | bytes accessed | tf_op | source)
XLA Modules:
  0.0 497.0 jit_solution(6133939188612458602)
XLA Ops:
  1.4 4.9 collective-permute-start
  23.0 152.0 %while.24 = (s32[]{:T(128)}, f32[5,20,128]{2,1,0:T(8,128)}, f32[5,20,128]{2,1,0:T(8,128)}, s32[5,128]{1,0:T(8,128)S(1)}, f32[20,416]{0,1:T(8,128)}, /*index=5*/b...) while((s32[]{:T(128)}, f32[5,20,128]{2,1,0:T(8,128)}, ...), condition=%wide.region_1.4_spmd, body=%wide.region_0.3_spmd.sunk | while | flops 32287744 | bytes 16952436 | solution.py:128
  27.2 4.8 stack.53
  32.7 5.4 %stack.52 = f32[10,128,256]{2,0,1:T(8,128)} concatenate(f32[1,128,256]{2,0,1:T(1,128)S(1)} %broadcast.300, f32[1,128,256]{2,0,1:T(1,128)} %get-tuple-element.348, f32[1,128,256]{2,0,1:T(1,128)} %get-tuple-element.349, f32[1,128,256]{2,0,1:T(1,128)S(1)} %get-tuple-element.350, f32[1,128,256]{2,0,1:T(1,128)S(1)} %get-tuple-element.351, f32[1,128,256]{2,0,1:T(1,128)S(1)} %get-tuple-element.352, ...), dimensions={0} | concatenate | bytes 2621440 | tf_op jit(solution)/shard_map/while/body/eval_jaxpr/stack | solution.py:34
  57.6 4.8 stack.53
  63.1 5.4 %stack.52 = f32[10,128,256]{2,0,1:T(8,128)} concatenate(f32[1,128,256]{2,0,1:T(1,128)S(1)} %broadcast.300, f32[1,128,256]{2,0,1:T(1,128)} %get-tuple-element.348, f32[1,128,256]{2,0,1:T(1,128)} %get-tuple-element.349, f32[1,128,256]{2,0,1:T(1,128)S(1)} %get-tuple-element.350, f32[1,128,256]{2,0,1:T(1,128)S(1)} %get-tuple-element.351, f32[1,128,256]{2,0,1:T(1,128)S(1)} %get-tuple-element.352, ...), dimensions={0} | concatenate | bytes 2621440 | tf_op jit(solution)/shard_map/while/body/eval_jaxpr/stack | solution.py:34
  87.9 4.8 stack.53
  93.5 5.4 %stack.52 = f32[10,128,256]{2,0,1:T(8,128)} concatenate(f32[1,128,256]{2,0,1:T(1,128)S(1)} %broadcast.300, f32[1,128,256]{2,0,1:T(1,128)} %get-tuple-element.348, f32[1,128,256]{2,0,1:T(1,128)} %get-tuple-element.349, f32[1,128,256]{2,0,1:T(1,128)S(1)} %get-tuple-element.350, f32[1,128,256]{2,0,1:T(1,128)S(1)} %get-tuple-element.351, f32[1,128,256]{2,0,1:T(1,128)S(1)} %get-tuple-element.352, ...), dimensions={0} | concatenate | bytes 2621440 | tf_op jit(solution)/shard_map/while/body/eval_jaxpr/stack | solution.py:34
  118.3 4.8 stack.53
  123.9 5.4 %stack.52 = f32[10,128,256]{2,0,1:T(8,128)} concatenate(f32[1,128,256]{2,0,1:T(1,128)S(1)} %broadcast.300, f32[1,128,256]{2,0,1:T(1,128)} %get-tuple-element.348, f32[1,128,256]{2,0,1:T(1,128)} %get-tuple-element.349, f32[1,128,256]{2,0,1:T(1,128)S(1)} %get-tuple-element.350, f32[1,128,256]{2,0,1:T(1,128)S(1)} %get-tuple-element.351, f32[1,128,256]{2,0,1:T(1,128)S(1)} %get-tuple-element.352, ...), dimensions={0} | concatenate | bytes 2621440 | tf_op jit(solution)/shard_map/while/body/eval_jaxpr/stack | solution.py:34
  154.3 5.4 %stack.52 = f32[10,128,256]{2,0,1:T(8,128)} concatenate(f32[1,128,256]{2,0,1:T(1,128)S(1)} %broadcast.300, f32[1,128,256]{2,0,1:T(1,128)} %get-tuple-element.348, f32[1,128,256]{2,0,1:T(1,128)} %get-tuple-element.349, f32[1,128,256]{2,0,1:T(1,128)S(1)} %get-tuple-element.350, f32[1,128,256]{2,0,1:T(1,128)S(1)} %get-tuple-element.351, f32[1,128,256]{2,0,1:T(1,128)S(1)} %get-tuple-element.352, ...), dimensions={0} | concatenate | bytes 2621440 | tf_op jit(solution)/shard_map/while/body/eval_jaxpr/stack | solution.py:34
  177.2 6.4 %scatter_custom_fusion = f32[20,416]{0,1:T(8,128)S(1)} fusion(s32[640]{0:T(1024)} %fusion.40, f32[640,20]{1,0:T(8,128)S(1)} %copy.78, f32[]{:T(128)} %constant.56.clone.1), kind=kCustom, calls=%fused_computation.104 | custom fusion | flops 12800 | bytes 33792 | tf_op jit(solution)/shard_map/scatter-add | solution.py:134
  183.6 6.1 %scatter_fusion = f32[20,416]{0,1:T(8,128)S(1)} fusion(f32[20,416]{0,1:T(8,128)S(1)} %scatter_custom_fusion, s32[640]{0:T(1024)S(1)} %fusion.41, f32[640,20]{1,0:T(8,128)S(1)} %copy.80), kind=kCustom, calls=%fused_computation.9 | custom fusion | flops 12800 | bytes 156160 | tf_op jit(solution)/shard_map/scatter-add | solution.py:134
  206.6 5.1 %collective-permute-start.8 = (f32[20,128]{0,1:T(8,128)S(1)}, f32[20,128]{0,1:T(8,128)S(1)}, u32[]{:S(2)}, u32[]{:S(2)}) collective-permute-start(f32[20,128]{0,1:T(8,128)S(1)} %bitcast_subtract_fusion), channel_id=1, source_target_pairs={{0,4},{4,8},{8,12},{12,16},{16,20},{20,24},{24,28},{28,32},{32,36}... | collective-permute-start | bytes 30728 | tf_op jit(solution)/shard_map/ppermute | solution.py:13
  225.3 152.0 %while.25 = (s32[]{:T(128)}, f32[5,20,128]{2,1,0:T(8,128)}, f32[5,20,128]{2,1,0:T(8,128)}, s32[5,128]{1,0:T(8,128)S(1)}, f32[20,416]{0,1:T(8,128)}, /*index=5*/b...) while((s32[]{:T(128)}, f32[5,20,128]{2,1,0:T(8,128)}, ...), condition=%wide.region_9.12_spmd, body=%wide.region_8.11_spmd.sunk | while | flops 32287744 | bytes 16952436 | solution.py:128
  235.1 5.4 %stack.70 = f32[10,128,256]{2,0,1:T(8,128)} concatenate(f32[1,128,256]{2,0,1:T(1,128)S(1)} %broadcast.309, f32[1,128,256]{2,0,1:T(1,128)} %get-tuple-element.377, f32[1,128,256]{2,0,1:T(1,128)} %get-tuple-element.378, f32[1,128,256]{2,0,1:T(1,128)S(1)} %get-tuple-element.379, f32[1,128,256]{2,0,1:T(1,128)S(1)} %get-tuple-element.380, f32[1,128,256]{2,0,1:T(1,128)S(1)} %get-tuple-element.381, ...), dimensions={0} | concatenate | bytes 2621440 | tf_op jit(solution)/shard_map/while/body/eval_jaxpr/stack | solution.py:34
  259.9 4.8 stack.71
  265.5 5.4 %stack.70 = f32[10,128,256]{2,0,1:T(8,128)} concatenate(f32[1,128,256]{2,0,1:T(1,128)S(1)} %broadcast.309, f32[1,128,256]{2,0,1:T(1,128)} %get-tuple-element.377, f32[1,128,256]{2,0,1:T(1,128)} %get-tuple-element.378, f32[1,128,256]{2,0,1:T(1,128)S(1)} %get-tuple-element.379, f32[1,128,256]{2,0,1:T(1,128)S(1)} %get-tuple-element.380, f32[1,128,256]{2,0,1:T(1,128)S(1)} %get-tuple-element.381, ...), dimensions={0} | concatenate | bytes 2621440 | tf_op jit(solution)/shard_map/while/body/eval_jaxpr/stack | solution.py:34
  295.9 5.4 %stack.70 = f32[10,128,256]{2,0,1:T(8,128)} concatenate(f32[1,128,256]{2,0,1:T(1,128)S(1)} %broadcast.309, f32[1,128,256]{2,0,1:T(1,128)} %get-tuple-element.377, f32[1,128,256]{2,0,1:T(1,128)} %get-tuple-element.378, f32[1,128,256]{2,0,1:T(1,128)S(1)} %get-tuple-element.379, f32[1,128,256]{2,0,1:T(1,128)S(1)} %get-tuple-element.380, f32[1,128,256]{2,0,1:T(1,128)S(1)} %get-tuple-element.381, ...), dimensions={0} | concatenate | bytes 2621440 | tf_op jit(solution)/shard_map/while/body/eval_jaxpr/stack | solution.py:34
  326.2 5.4 %stack.70 = f32[10,128,256]{2,0,1:T(8,128)} concatenate(f32[1,128,256]{2,0,1:T(1,128)S(1)} %broadcast.309, f32[1,128,256]{2,0,1:T(1,128)} %get-tuple-element.377, f32[1,128,256]{2,0,1:T(1,128)} %get-tuple-element.378, f32[1,128,256]{2,0,1:T(1,128)S(1)} %get-tuple-element.379, f32[1,128,256]{2,0,1:T(1,128)S(1)} %get-tuple-element.380, f32[1,128,256]{2,0,1:T(1,128)S(1)} %get-tuple-element.381, ...), dimensions={0} | concatenate | bytes 2621440 | tf_op jit(solution)/shard_map/while/body/eval_jaxpr/stack | solution.py:34
  356.6 5.4 %stack.70 = f32[10,128,256]{2,0,1:T(8,128)} concatenate(f32[1,128,256]{2,0,1:T(1,128)S(1)} %broadcast.309, f32[1,128,256]{2,0,1:T(1,128)} %get-tuple-element.377, f32[1,128,256]{2,0,1:T(1,128)} %get-tuple-element.378, f32[1,128,256]{2,0,1:T(1,128)S(1)} %get-tuple-element.379, f32[1,128,256]{2,0,1:T(1,128)S(1)} %get-tuple-element.380, f32[1,128,256]{2,0,1:T(1,128)S(1)} %get-tuple-element.381, ...), dimensions={0} | concatenate | bytes 2621440 | tf_op jit(solution)/shard_map/while/body/eval_jaxpr/stack | solution.py:34
  379.5 6.4 %scatter_custom_fusion.4 = f32[20,416]{0,1:T(8,128)S(1)} fusion(s32[640]{0:T(1024)} %fusion.40, f32[640,20]{1,0:T(8,128)S(1)} %copy.89, f32[]{:T(128)} %constant.56.clone.1), kind=kCustom, calls=%fused_computation.102 | custom fusion | flops 12800 | bytes 33792 | tf_op jit(solution)/shard_map/scatter-add | solution.py:134
  385.9 6.1 %scatter_fusion.1 = f32[20,416]{0,1:T(8,128)S(1)} fusion(f32[20,416]{0,1:T(8,128)S(1)} %scatter_custom_fusion.4, s32[640]{0:T(1024)S(1)} %fusion.41, f32[640,20]{1,0:T(8,128)S(1)} %copy.91), kind=kCustom, calls=%fused_computation.13 | custom fusion | flops 12800 | bytes 156160 | tf_op jit(solution)/shard_map/scatter-add | solution.py:134
  409.4 84.8 %all-reduce = (f32[]{:T(128)}, f32[]{:T(128)}) all-reduce(f32[]{:T(128)} %get-tuple-element.119, f32[]{:T(128)} %get-tuple-element.118), channel_id=1, replica_groups=mesh['sec'=64,'reg'=4] {'sec','reg'}, use_global_device_ids=true, to_apply=%region_7.10 | all-reduce | flops 2 | bytes 16 | tf_op jit(solution)/shard_map/psum | solution.py:139
  (400 shorter events, 295.1 us)
Async XLA Ops:
  1.4 12.7 %collective-permute-start = (f32[20,128]{0,1:T(8,128)S(1)}, f32[20,128]{0,1:T(8,128)S(1)}, u32[]{:S(2)}, u32[]{:S(2)}) collective-permute-start(f32[20,128]{0,1:T(8,128)S(1)} %bitcast.359), channel_id=1, source_target_pairs={{0,4},{4,8},{8,12},{12,16},{16,20},{20,24},{24,28},{28,32},{32,36}... | collective-permute-start | bytes 30728 | tf_op jit(solution)/shard_map/ppermute | solution.py:13
  7.8 12.7 %collective-permute-start.2 = (f32[1,20,16]{1,2,0:T(8,128)S(1)}, f32[1,20,16]{1,2,0:T(8,128)S(1)}, u32[]{:S(2)}, u32[]{:S(2)}) collective-permute-start(f32[1,20,16]{1,2,0:T(8,128)S(1)} %select_bitcast_fusion.7), channel_id=1, source_target_pairs={{0,1},{1,2},{2,3},{4,5},{5,6},{6,7},{8,9},{9,10},{10,11},{12,13},{... | collective-permute-start | bytes 3848 | tf_op jit(solution)/shard_map/ppermute | solution.py:23
  11.6 9.0 %collective-permute-start.3 = (f32[1,20,16]{1,2,0:T(8,128)S(1)}, f32[1,20,16]{1,2,0:T(8,128)S(1)}, u32[]{:S(2)}, u32[]{:S(2)}) collective-permute-start(f32[1,20,16]{1,2,0:T(8,128)S(1)} %select_bitcast_fusion.6), channel_id=1, source_target_pairs={{1,0},{2,1},{3,2},{5,4},{6,5},{7,6},{9,8},{10,9},{11,10},{13,12},{... | collective-permute-start | bytes 3848 | tf_op jit(solution)/shard_map/ppermute | solution.py:24
  14.2 6.5 %collective-permute-start.1 = (f32[20,128]{0,1:T(8,128)S(1)}, f32[20,128]{0,1:T(8,128)S(1)}, u32[]{:S(2)}, u32[]{:S(2)}) collective-permute-start(f32[20,128]{0,1:T(8,128)S(1)} %collective-permute-done), channel_id=1, source_target_pairs={{0,4},{4,8},{8,12},{12,16},{16,20},{20,24},{24,28},{28,32},{32,36}... | collective-permute-start | bytes 30728 | tf_op jit(solution)/shard_map/ppermute | solution.py:13
  175.0 27.8 %copy-start.3 = (f32[1,1,20,128]{2,3,1,0:T(8,128)S(1)}, f32[1,1,20,128]{2,3,1,0:T(8,128)}, u32[]{:S(2)}) copy-start(f32[1,1,20,128]{2,3,1,0:T(8,128)} %copy-done.2) | copy-start | bytes 30724
  175.9 36.4 %copy-start.13 = (pred[16]{0:T(512)(128)(4,1)S(1)}, pred[16]{0:T(512)(128)(4,1)}, u32[]{:S(2)}) copy-start(pred[16]{0:T(512)(128)(4,1)} %copy-done.12) | copy-start | bytes 52
  175.9 42.5 %copy-start.11 = (pred[16]{0:T(512)(128)(4,1)S(1)}, pred[16]{0:T(512)(128)(4,1)}, u32[]{:S(2)}) copy-start(pred[16]{0:T(512)(128)(4,1)} %copy-done.10) | copy-start | bytes 52
  189.7 5.6 %collective-permute-start.4 = (f32[20,128]{0,1:T(8,128)S(1)}, f32[20,128]{0,1:T(8,128)S(1)}, u32[]{:S(2)}, u32[]{:S(2)}) collective-permute-start(f32[20,128]{0,1:T(8,128)S(1)} %slice.106), channel_id=1, source_target_pairs={{4,0},{8,4},{12,8},{16,12},{20,16},{24,20},{28,24},{32,28},{36,32}... | collective-permute-start | bytes 30728 | tf_op jit(solution)/shard_map/ppermute | solution.py:13
  191.9 33.4 %copy-start.15 = (s32[16]{0:T(128)}, s32[16]{0:T(128)S(1)}, u32[]{:S(2)}) copy-start(s32[16]{0:T(128)S(1)} %get-tuple-element.210) | copy-start | bytes 196
  191.9 33.4 %copy-start.16 = (s32[16]{0:T(128)}, s32[16]{0:T(128)S(1)}, u32[]{:S(2)}) copy-start(s32[16]{0:T(128)S(1)} %get-tuple-element.211) | copy-start | bytes 196
  192.0 33.3 %copy-start.5 = (f32[1,1,20,128]{2,3,1,0:T(8,128)}, f32[1,1,20,128]{2,3,1,0:T(8,128)S(1)}, u32[]{:S(2)}) copy-start(f32[1,1,20,128]{2,3,1,0:T(8,128)S(1)} %copy.81) | copy-start | bytes 30724
  195.3 7.5 %collective-permute-start.5 = (f32[20,128]{0,1:T(8,128)S(1)}, f32[20,128]{0,1:T(8,128)S(1)}, u32[]{:S(2)}, u32[]{:S(2)}) collective-permute-start(f32[20,128]{0,1:T(8,128)S(1)} %slice_add_fusion.2), channel_id=1, source_target_pairs={{4,0},{8,4},{12,8},{16,12},{20,16},{24,20},{28,24},{32,28},{36,32}... | collective-permute-start | bytes 30728 | tf_op jit(solution)/shard_map/ppermute | solution.py:13
  197.2 5.6 %collective-permute-start.6 = (f32[1,20,16]{1,2,0:T(8,128)S(1)}, f32[1,20,16]{1,2,0:T(8,128)S(1)}, u32[]{:S(2)}, u32[]{:S(2)}) collective-permute-start(f32[1,20,16]{1,2,0:T(8,128)S(1)} %get-tuple-element.207), channel_id=1, source_target_pairs={{0,1},{1,2},{2,3},{4,5},{5,6},{6,7},{8,9},{9,10},{10,11},{12,13},{... | collective-permute-start | bytes 3848 | tf_op jit(solution)/shard_map/ppermute | solution.py:23
  201.5 4.4 collective-permute-start.7
  206.6 9.5 %collective-permute-start.8 = (f32[20,128]{0,1:T(8,128)S(1)}, f32[20,128]{0,1:T(8,128)S(1)}, u32[]{:S(2)}, u32[]{:S(2)}) collective-permute-start(f32[20,128]{0,1:T(8,128)S(1)} %bitcast_subtract_fusion), channel_id=1, source_target_pairs={{0,4},{4,8},{8,12},{12,16},{16,20},{20,24},{24,28},{28,32},{32,36}... | collective-permute-start | bytes 30728 | tf_op jit(solution)/shard_map/ppermute | solution.py:13
  213.0 6.8 %collective-permute-start.10 = (f32[1,20,16]{1,2,0:T(8,128)S(1)}, f32[1,20,16]{1,2,0:T(8,128)S(1)}, u32[]{:S(2)}, u32[]{:S(2)}) collective-permute-start(f32[1,20,16]{1,2,0:T(8,128)S(1)} %select_bitcast_fusion.5), channel_id=1, source_target_pairs={{0,1},{1,2},{2,3},{4,5},{5,6},{6,7},{8,9},{9,10},{10,11},{12,13},{... | collective-permute-start | bytes 3848 | tf_op jit(solution)/shard_map/ppermute | solution.py:23
  216.2 6.8 %collective-permute-start.9 = (f32[20,128]{0,1:T(8,128)S(1)}, f32[20,128]{0,1:T(8,128)S(1)}, u32[]{:S(2)}, u32[]{:S(2)}) collective-permute-start(f32[20,128]{0,1:T(8,128)S(1)} %collective-permute-done.8), channel_id=1, source_target_pairs={{0,4},{4,8},{8,12},{12,16},{16,20},{20,24},{24,28},{28,32},{32,36}... | collective-permute-start | bytes 30728 | tf_op jit(solution)/shard_map/ppermute | solution.py:13
  218.5 4.4 collective-permute-start.11
  377.3 27.6 %copy-start.6 = (f32[1,1,20,128]{2,3,1,0:T(8,128)S(1)}, f32[1,1,20,128]{2,3,1,0:T(8,128)}, u32[]{:S(2)}) copy-start(f32[1,1,20,128]{2,3,1,0:T(8,128)} %copy-done.5) | copy-start | bytes 30724
  377.3 118.3 %copy-start.4 = (f32[1,1,20,128]{2,3,1,0:T(8,128)S(1)}, f32[1,1,20,128]{2,3,1,0:T(8,128)}, u32[]{:S(2)}) copy-start(f32[1,1,20,128]{2,3,1,0:T(8,128)} %copy-done.2) | copy-start | bytes 30724
  392.0 6.8 %collective-permute-start.12 = (f32[20,128]{0,1:T(8,128)S(1)}, f32[20,128]{0,1:T(8,128)S(1)}, u32[]{:S(2)}, u32[]{:S(2)}) collective-permute-start(f32[20,128]{0,1:T(8,128)S(1)} %slice.111), channel_id=1, source_target_pairs={{4,0},{8,4},{12,8},{16,12},{20,16},{24,20},{28,24},{32,28},{36,32}... | collective-permute-start | bytes 30728 | tf_op jit(solution)/shard_map/ppermute | solution.py:13
  398.8 6.1 %collective-permute-start.13 = (f32[20,128]{0,1:T(8,128)S(1)}, f32[20,128]{0,1:T(8,128)S(1)}, u32[]{:S(2)}, u32[]{:S(2)}) collective-permute-start(f32[20,128]{0,1:T(8,128)S(1)} %slice_add_fusion), channel_id=1, source_target_pairs={{4,0},{8,4},{12,8},{16,12},{20,16},{24,20},{28,24},{32,28},{36,32}... | collective-permute-start | bytes 30728 | tf_op jit(solution)/shard_map/ppermute | solution.py:13
  400.8 4.2 collective-permute-start.14
  403.6 4.4 collective-permute-start.15
  (9 other events, 145.4 us)
where the time goes:
time: 506 us; the launch traced here: 497 us
  local copies, waits for them, and re-layouts  185 us (37%)
  matrix products  93.3 us (18%)
  blocking collectives  84.8 us (17%)
  other arithmetic  74.4 us (15%)
  starting transfers between devices  42.1 us (8%)
  waiting for transfers between devices  14.2 us (3%)
    another operation x20, local copies, waits for them, and re-layouts, monomials(): jnp.stack([constant, across, upward, square_a, mixed, square_b, square_a...  102 us
    psum x1, blocking collectives, global_dot(): return lax.psum(value, ('sec', 'reg'))  84.8 us
    dot_general x10, matrix products, block_terms(): jnp.einsum('mpk,cpk->cmp', basis_a, mismatch, precision=FULL_PRECISION)  34.1 us
    dot_general x10, matrix products, block_terms(): jnp.einsum('mpk,cmp->cpk', basis_a, own, precision=FULL_PRECISION)  27.9 us
    scatter-add x4, other arithmetic, apply_normal(): products = products.at[:, first].add(to_own).at[:, second].add(to_other)  25 us
    ppermute x8, starting transfers between devices, shifted(): return lax.ppermute(array, axis, pairs)  23.6 us
    mul x10, other arithmetic, monomials(): square_b * upward  19.2 us
    dot_general x10, matrix products, block_terms(): jnp.einsum('mpk,cpk->cmp', basis_b, mismatch, precision=FULL_PRECISION)  18.3 us
  transfers between devices with their start and end apart: 16, of which 5 were waited for; matrix products, arithmetic and copies ran while one was open for 2% of the time, Pallas kernels for 0%

commit v1 on v0

--- a/solution.py
+++ b/solution.py
@@ -136,7 +136,7 @@
 
 
 def global_dot(value):
-    return lax.psum(value, ("sec", "reg"))
+    return lax.psum(lax.psum(value, "sec"), "reg")
 
 
 def on_device(

time: 506 us -> 559 us (1.10)
  the two profiles are of different devices: /device:TPU:1 before, /device:TPU:2 now
where the time goes in v1:
time: 559 us; the launch traced here: 550 us
  local copies, waits for them, and re-layouts  185 us (33%)
  blocking collectives  142 us (25%)
  matrix products  93.3 us (17%)
  other arithmetic  74.5 us (13%)
  starting transfers between devices  42.6 us (8%)
  waiting for transfers between devices  9.47 us (2%)
    psum x2, blocking collectives, global_dot(): return lax.psum(lax.psum(value, 'sec'), 'reg')  142 us
    another operation x20, local copies, waits for them, and re-layouts, monomials(): jnp.stack([constant, across, upward, square_a, mixed, square_b, square_a...  102 us
    dot_general x10, matrix products, block_terms(): jnp.einsum('mpk,cpk->cmp', basis_a, mismatch, precision=FULL_PRECISION)  34.1 us
    dot_general x10, matrix products, block_terms(): jnp.einsum('mpk,cmp->cpk', basis_a, own, precision=FULL_PRECISION)  27.9 us
    scatter-add x4, other arithmetic, apply_normal(): products = products.at[:, first].add(to_own).at[:, second].add(to_other)  25 us
    ppermute x8, starting transfers between devices, shifted(): return lax.ppermute(array, axis, pairs)  19.3 us
    mul x10, other arithmetic, monomials(): square_b * upward  19.3 us
    dot_general x10, matrix products, block_terms(): jnp.einsum('mpk,cpk->cmp', basis_b, mismatch, precision=FULL_PRECISION)  18.3 us
  transfers between devices with their start and end apart: 16, of which 5 were waited for; matrix products, arithmetic and copies ran while one was open for 2% of the time, Pallas kernels for 0%

profile of v1, /device:TPU:2, one launch (start us, length us, event | category | flops | bytes accessed | tf_op | source)
XLA Modules:
  0.0 549.9 jit_solution(1911731957454355684)
XLA Ops:
  22.6 152.0 %while.24 = (s32[]{:T(128)}, f32[5,20,128]{2,1,0:T(8,128)}, f32[5,20,128]{2,1,0:T(8,128)}, s32[5,128]{1,0:T(8,128)S(1)}, f32[20,416]{0,1:T(8,128)}, /*index=5*/b...) while((s32[]{:T(128)}, f32[5,20,128]{2,1,0:T(8,128)}, ...), condition=%wide.region_1.4_spmd, body=%wide.region_0.3_spmd.sunk | while | flops 32287744 | bytes 16952436 | solution.py:128
  26.8 4.8 stack.53
  32.4 5.4 stack.52
  57.2 4.8 stack.53
  62.8 5.4 stack.52
  87.6 4.8 stack.53
  93.2 5.4 stack.52
  118.0 4.8 stack.53
  123.5 5.4 stack.52
  153.9 5.4 stack.52
  176.8 6.4 %scatter_custom_fusion = f32[20,416]{0,1:T(8,128)S(1)} fusion(s32[640]{0:T(1024)} %fusion.40, f32[640,20]{1,0:T(8,128)S(1)} %copy.78, f32[]{:T(128)} %constant.56.clone.1), kind=kCustom, calls=%fused_computation.104 | custom fusion | flops 12800 | bytes 33792 | tf_op jit(solution)/shard_map/scatter-add | solution.py:134
  183.2 6.1 %scatter_fusion = f32[20,416]{0,1:T(8,128)S(1)} fusion(f32[20,416]{0,1:T(8,128)S(1)} %scatter_custom_fusion, s32[640]{0:T(1024)S(1)} %fusion.41, f32[640,20]{1,0:T(8,128)S(1)} %copy.80), kind=kCustom, calls=%fused_computation.9 | custom fusion | flops 12800 | bytes 156160 | tf_op jit(solution)/shard_map/scatter-add | solution.py:134
  224.9 152.0 %while.25 = (s32[]{:T(128)}, f32[5,20,128]{2,1,0:T(8,128)}, f32[5,20,128]{2,1,0:T(8,128)}, s32[5,128]{1,0:T(8,128)S(1)}, f32[20,416]{0,1:T(8,128)}, /*index=5*/b...) while((s32[]{:T(128)}, f32[5,20,128]{2,1,0:T(8,128)}, ...), condition=%wide.region_10.13_spmd, body=%wide.region_9.12_spmd.sunk | while | flops 32287744 | bytes 16952436 | solution.py:128
  234.7 5.4 stack.70
  265.1 5.4 stack.70
  289.9 4.8 stack.71
  295.5 5.4 stack.70
  320.3 4.8 stack.71
  325.9 5.4 stack.70
  356.3 5.4 stack.70
  379.1 6.4 %scatter_custom_fusion.4 = f32[20,416]{0,1:T(8,128)S(1)} fusion(s32[640]{0:T(1024)} %fusion.40, f32[640,20]{1,0:T(8,128)S(1)} %copy.89, f32[]{:T(128)} %constant.56.clone.1), kind=kCustom, calls=%fused_computation.102 | custom fusion | flops 12800 | bytes 33792 | tf_op jit(solution)/shard_map/scatter-add | solution.py:134
  385.5 6.1 %scatter_fusion.1 = f32[20,416]{0,1:T(8,128)S(1)} fusion(f32[20,416]{0,1:T(8,128)S(1)} %scatter_custom_fusion.4, s32[640]{0:T(1024)S(1)} %fusion.41, f32[640,20]{1,0:T(8,128)S(1)} %copy.91), kind=kCustom, calls=%fused_computation.13 | custom fusion | flops 12800 | bytes 156160 | tf_op jit(solution)/shard_map/scatter-add | solution.py:134
  405.3 131.9 %all-reduce = (f32[]{:T(128)}, f32[]{:T(128)}) all-reduce(f32[]{:T(128)} %get-tuple-element.119, f32[]{:T(128)} %get-tuple-element.118), channel_id=1, replica_groups=mesh['sec'=64,'reg'=4] {'sec'}, use_global_device_ids=true, to_apply=%region_7.10 | all-reduce | flops 2 | bytes 16 | tf_op jit(solution)/shard_map/psum | solution.py:139
  537.2 10.0 %all-reduce.1 = (f32[]{:T(128)}, f32[]{:T(128)}) all-reduce(f32[]{:T(128)} %get-tuple-element.152, f32[]{:T(128)} %get-tuple-element.153), channel_id=1, replica_groups=mesh['sec'=64,'reg'=4] {'reg'}, use_global_device_ids=true, to_apply=%region_8.11 | all-reduce | flops 2 | bytes 16 | tf_op jit(solution)/shard_map/psum | solution.py:139
  (401 shorter events, 296.2 us)
Async XLA Ops:
  1.4 11.0 %collective-permute-start = (f32[20,128]{0,1:T(8,128)S(1)}, f32[20,128]{0,1:T(8,128)S(1)}, u32[]{:S(2)}, u32[]{:S(2)}) collective-permute-start(f32[20,128]{0,1:T(8,128)S(1)} %bitcast.359), channel_id=1, source_target_pairs={{0,4},{4,8},{8,12},{12,16},{16,20},{20,24},{24,28},{28,32},{32,36}... | collective-permute-start | bytes 30728 | tf_op jit(solution)/shard_map/ppermute | solution.py:13
  4.6 15.4 %collective-permute-start.2 = (f32[1,20,16]{1,2,0:T(8,128)S(1)}, f32[1,20,16]{1,2,0:T(8,128)S(1)}, u32[]{:S(2)}, u32[]{:S(2)}) collective-permute-start(f32[1,20,16]{1,2,0:T(8,128)S(1)} %select_bitcast_fusion.7), channel_id=1, source_target_pairs={{0,1},{1,2},{2,3},{4,5},{5,6},{6,7},{8,9},{9,10},{10,11},{12,13},{... | collective-permute-start | bytes 3848 | tf_op jit(solution)/shard_map/ppermute | solution.py:23
  8.7 11.5 %collective-permute-start.3 = (f32[1,20,16]{1,2,0:T(8,128)S(1)}, f32[1,20,16]{1,2,0:T(8,128)S(1)}, u32[]{:S(2)}, u32[]{:S(2)}) collective-permute-start(f32[1,20,16]{1,2,0:T(8,128)S(1)} %select_bitcast_fusion.6), channel_id=1, source_target_pairs={{1,0},{2,1},{3,2},{5,4},{6,5},{7,6},{9,8},{10,9},{11,10},{13,12},{... | collective-permute-start | bytes 3848 | tf_op jit(solution)/shard_map/ppermute | solution.py:24
  12.4 7.9 %collective-permute-start.1 = (f32[20,128]{0,1:T(8,128)S(1)}, f32[20,128]{0,1:T(8,128)S(1)}, u32[]{:S(2)}, u32[]{:S(2)}) collective-permute-start(f32[20,128]{0,1:T(8,128)S(1)} %collective-permute-done), channel_id=1, source_target_pairs={{0,4},{4,8},{8,12},{12,16},{16,20},{20,24},{24,28},{28,32},{32,36}... | collective-permute-start | bytes 30728 | tf_op jit(solution)/shard_map/ppermute | solution.py:13
  174.6 25.1 %copy-start.3 = (f32[1,1,20,128]{2,3,1,0:T(8,128)S(1)}, f32[1,1,20,128]{2,3,1,0:T(8,128)}, u32[]{:S(2)}) copy-start(f32[1,1,20,128]{2,3,1,0:T(8,128)} %copy-done.2) | copy-start | bytes 30724
  175.5 32.7 %copy-start.13 = (pred[16]{0:T(512)(128)(4,1)S(1)}, pred[16]{0:T(512)(128)(4,1)}, u32[]{:S(2)}) copy-start(pred[16]{0:T(512)(128)(4,1)} %copy-done.12) | copy-start | bytes 52
  175.5 41.3 %copy-start.11 = (pred[16]{0:T(512)(128)(4,1)S(1)}, pred[16]{0:T(512)(128)(4,1)}, u32[]{:S(2)}) copy-start(pred[16]{0:T(512)(128)(4,1)} %copy-done.10) | copy-start | bytes 52
  189.3 3.2 collective-permute-start.4
  190.6 34.3 %copy-start.15 = (s32[16]{0:T(128)}, s32[16]{0:T(128)S(1)}, u32[]{:S(2)}) copy-start(s32[16]{0:T(128)S(1)} %get-tuple-element.212) | copy-start | bytes 196
  190.7 34.2 %copy-start.16 = (s32[16]{0:T(128)}, s32[16]{0:T(128)S(1)}, u32[]{:S(2)}) copy-start(s32[16]{0:T(128)S(1)} %get-tuple-element.213) | copy-start | bytes 196
  190.8 34.1 %copy-start.5 = (f32[1,1,20,128]{2,3,1,0:T(8,128)}, f32[1,1,20,128]{2,3,1,0:T(8,128)S(1)}, u32[]{:S(2)}) copy-start(f32[1,1,20,128]{2,3,1,0:T(8,128)S(1)} %copy.81) | copy-start | bytes 30724
  192.6 7.2 %collective-permute-start.5 = (f32[20,128]{0,1:T(8,128)S(1)}, f32[20,128]{0,1:T(8,128)S(1)}, u32[]{:S(2)}, u32[]{:S(2)}) collective-permute-start(f32[20,128]{0,1:T(8,128)S(1)} %slice_add_fusion.2), channel_id=1, source_target_pairs={{4,0},{8,4},{12,8},{16,12},{20,16},{24,20},{28,24},{32,28},{36,32}... | collective-permute-start | bytes 30728 | tf_op jit(solution)/shard_map/ppermute | solution.py:13
  193.9 5.9 %collective-permute-start.6 = (f32[1,20,16]{1,2,0:T(8,128)S(1)}, f32[1,20,16]{1,2,0:T(8,128)S(1)}, u32[]{:S(2)}, u32[]{:S(2)}) collective-permute-start(f32[1,20,16]{1,2,0:T(8,128)S(1)} %get-tuple-element.209), channel_id=1, source_target_pairs={{0,1},{1,2},{2,3},{4,5},{5,6},{6,7},{8,9},{9,10},{10,11},{12,13},{... | collective-permute-start | bytes 3848 | tf_op jit(solution)/shard_map/ppermute | solution.py:23
  197.3 5.5 %collective-permute-start.7 = (f32[1,20,16]{1,2,0:T(8,128)S(1)}, f32[1,20,16]{1,2,0:T(8,128)S(1)}, u32[]{:S(2)}, u32[]{:S(2)}) collective-permute-start(f32[1,20,16]{1,2,0:T(8,128)S(1)} %get-tuple-element.208), channel_id=1, source_target_pairs={{1,0},{2,1},{3,2},{5,4},{6,5},{7,6},{9,8},{10,9},{11,10},{13,12},{... | collective-permute-start | bytes 3848 | tf_op jit(solution)/shard_map/ppermute | solution.py:24
  203.5 8.5 %collective-permute-start.8 = (f32[20,128]{0,1:T(8,128)S(1)}, f32[20,128]{0,1:T(8,128)S(1)}, u32[]{:S(2)}, u32[]{:S(2)}) collective-permute-start(f32[20,128]{0,1:T(8,128)S(1)} %bitcast_subtract_fusion), channel_id=1, source_target_pairs={{0,4},{4,8},{8,12},{12,16},{16,20},{20,24},{24,28},{28,32},{32,36}... | collective-permute-start | bytes 30728 | tf_op jit(solution)/shard_map/ppermute | solution.py:13
  208.9 10.8 %collective-permute-start.10 = (f32[1,20,16]{1,2,0:T(8,128)S(1)}, f32[1,20,16]{1,2,0:T(8,128)S(1)}, u32[]{:S(2)}, u32[]{:S(2)}) collective-permute-start(f32[1,20,16]{1,2,0:T(8,128)S(1)} %select_bitcast_fusion.5), channel_id=1, source_target_pairs={{0,1},{1,2},{2,3},{4,5},{5,6},{6,7},{8,9},{9,10},{10,11},{12,13},{... | collective-permute-start | bytes 3848 | tf_op jit(solution)/shard_map/ppermute | solution.py:23
  212.0 10.6 %collective-permute-start.9 = (f32[20,128]{0,1:T(8,128)S(1)}, f32[20,128]{0,1:T(8,128)S(1)}, u32[]{:S(2)}, u32[]{:S(2)}) collective-permute-start(f32[20,128]{0,1:T(8,128)S(1)} %collective-permute-done.8), channel_id=1, source_target_pairs={{0,4},{4,8},{8,12},{12,16},{16,20},{20,24},{24,28},{28,32},{32,36}... | collective-permute-start | bytes 30728 | tf_op jit(solution)/shard_map/ppermute | solution.py:13
  216.9 5.5 %collective-permute-start.11 = (f32[1,20,16]{1,2,0:T(8,128)S(1)}, f32[1,20,16]{1,2,0:T(8,128)S(1)}, u32[]{:S(2)}, u32[]{:S(2)}) collective-permute-start(f32[1,20,16]{1,2,0:T(8,128)S(1)} %select_bitcast_fusion.4), channel_id=1, source_target_pairs={{1,0},{2,1},{3,2},{5,4},{6,5},{7,6},{9,8},{10,9},{11,10},{13,12},{... | collective-permute-start | bytes 3848 | tf_op jit(solution)/shard_map/ppermute | solution.py:24
  376.9 25.1 %copy-start.6 = (f32[1,1,20,128]{2,3,1,0:T(8,128)S(1)}, f32[1,1,20,128]{2,3,1,0:T(8,128)}, u32[]{:S(2)}) copy-start(f32[1,1,20,128]{2,3,1,0:T(8,128)} %copy-done.5) | copy-start | bytes 30724
  376.9 171.6 %copy-start.4 = (f32[1,1,20,128]{2,3,1,0:T(8,128)S(1)}, f32[1,1,20,128]{2,3,1,0:T(8,128)}, u32[]{:S(2)}) copy-start(f32[1,1,20,128]{2,3,1,0:T(8,128)} %copy-done.2) | copy-start | bytes 30724
  391.6 3.1 collective-permute-start.12
  394.8 7.2 %collective-permute-start.13 = (f32[20,128]{0,1:T(8,128)S(1)}, f32[20,128]{0,1:T(8,128)S(1)}, u32[]{:S(2)}, u32[]{:S(2)}) collective-permute-start(f32[20,128]{0,1:T(8,128)S(1)} %slice_add_fusion), channel_id=1, source_target_pairs={{4,0},{8,4},{12,8},{16,12},{20,16},{24,20},{28,24},{32,28},{36,32}... | collective-permute-start | bytes 30728 | tf_op jit(solution)/shard_map/ppermute | solution.py:13
  396.1 5.9 %collective-permute-start.14 = (f32[1,20,16]{1,2,0:T(8,128)S(1)}, f32[1,20,16]{1,2,0:T(8,128)S(1)}, u32[]{:S(2)}, u32[]{:S(2)}) collective-permute-start(f32[1,20,16]{1,2,0:T(8,128)S(1)} %get-tuple-element.207), channel_id=1, source_target_pairs={{0,1},{1,2},{2,3},{4,5},{5,6},{6,7},{8,9},{9,10},{10,11},{12,13},{... | collective-permute-start | bytes 3848 | tf_op jit(solution)/shard_map/ppermute | solution.py:23
  398.3 5.5 %collective-permute-start.15 = (f32[1,20,16]{1,2,0:T(8,128)S(1)}, f32[1,20,16]{1,2,0:T(8,128)S(1)}, u32[]{:S(2)}, u32[]{:S(2)}) collective-permute-start(f32[1,20,16]{1,2,0:T(8,128)S(1)} %get-tuple-element.206), channel_id=1, source_target_pairs={{1,0},{2,1},{3,2},{5,4},{6,5},{7,6},{9,8},{10,9},{11,10},{13,12},{... | collective-permute-start | bytes 3848 | tf_op jit(solution)/shard_map/ppermute | solution.py:24
  (9 other events, 148.2 us)
